TPU v7x, 32 devices: a whole 2x2x4 slice. The times are simulated.
32 devices in a mesh: cfg: 2 (over core), seq: 8 (over z, x), tile: 2 (over y).
Axes of the slice: x: 2, y: 2, z: 4, core: 2. Of those that a mesh axis runs over, the one named last changes fastest.
Arguments:
- section_input: bfloat16 [4, 128, 64, 384], P('tile', None, 'seq'), may hold values from -6 to 6
- norm_gain: float32 [384], replicated, may hold values from 0.5 to 1.5
- conv_weight: bfloat16 [384, 864], replicated, may hold values from -0.0625 to 0.0625
- conv_bias: float32 [32], replicated, may hold values from -3 to 3
- mean_weight: float32 [32, 16], replicated, may hold values from -1 to 1
- mean_bias: float32 [16], replicated, may hold values from -3 to 3
- noisy_tokens: bfloat16 [8192, 64], P(('seq', 'tile')), may hold values from -6 to 6
- mask_tokens: bfloat16 [8192, 128], P(('seq', 'tile')), may hold values from 0 to 1
- patch_weight: bfloat16 [64, 5120], replicated, may hold values from -0.75 to 0.75
- patch_bias: float32 [5120], replicated, may hold values from -3 to 3
- context_weight: bfloat16 [192, 5120], replicated, may hold values from -0.4375 to 0.4375
- context_bias: float32 [5120], replicated, may hold values from -3 to 3
- norm_shift: float32 [5120], replicated, may hold values from -3 to 3
- norm_scale: float32 [5120], replicated, may hold values from -3 to 3
Outputs:
- block_input: bfloat16 [8192, 5120], P(('seq', 'tile'))
All inputs are finite; a program needn't handle non-finite values.
Results may differ from a plain program's by a relative error of at most 0.004.
Values may be sent and summed in bfloat16 or wider, within the bound.
A program may use at most 128 MiB of HBM per device.

v0:
```python
import jax
import jax.numpy as jnp
from jax import lax
from jax.sharding import PartitionSpec as P

K = 3


def with_halo(x, sides, width):
    for axis, dim in sides:
        size, length = (lax.axis_size(axis), x.shape[dim])
        up = [(i, (i + 1) % size) for i in range(size - 1)]
        down = [(j, i) for i, j in up]
        last = lax.slice_in_dim(x, length - width, length, axis=dim)
        first = lax.slice_in_dim(x, 0, width, axis=dim)
        before = lax.ppermute(last, axis, up)
        after = lax.ppermute(first, axis, down)
        x = jnp.concatenate([before, x, after], axis=dim)
    return x


def from_behind(x, axis, by):
    length = lax.axis_size(axis)
    pairs = [(i, i + by) for i in range(length) if 0 <= i + by < length]
    return lax.ppermute(x, axis, pairs)


def body(
    section_input,
    norm_gain,
    conv_weight,
    conv_bias,
    mean_weight,
    mean_bias,
    noisy_tokens,
    mask_tokens,
    patch_weight,
    patch_bias,
    context_weight,
    context_bias,
    norm_shift,
    norm_scale,
):
    frames, height, columns, channels = section_input.shape
    values = section_input.astype(jnp.float32)
    energy = jnp.mean(values * values, axis=-1, keepdims=True)
    activation = jax.nn.silu(values * lax.rsqrt(energy + 1e-06) * norm_gain).astype(jnp.bfloat16)
    kernel = conv_weight.reshape(channels, K * K * K, -1)
    out_chans = kernel.shape[-1]
    share_width = out_chans // lax.axis_size("cfg")
    offset = lax.axis_index("cfg") * share_width
    kernel = lax.dynamic_slice_in_dim(kernel, offset, share_width, 2)
    conv_shift = lax.dynamic_slice_in_dim(conv_bias, offset, share_width, 0)
    head_weight = lax.dynamic_slice_in_dim(mean_weight, offset, share_width, 0)
    tap_matrix = kernel.reshape(channels, K * K * K * share_width)
    spread = jnp.dot(
        activation.reshape(-1, channels), tap_matrix, preferred_element_type=jnp.float32
    )
    spread = spread.reshape(frames, height, columns, K * K * K, share_width)
    extended = jnp.zeros((frames + 2, height + 2, columns + 2, share_width), jnp.float32)
    for step_t in range(K):
        for step_h in range(K):
            for step_w in range(K):
                tap_index = (step_t * K + step_h) * K + step_w
                pad_plan = (
                    (2 - step_t, step_t),
                    (2 - step_h, step_h),
                    (2 - step_w, step_w),
                    (0, 0),
                )
                extended = extended + jnp.pad(spread[:, :, :, tap_index], pad_plan)
    extended = extended[:, 1 : height + 1]
    spill_edges = jnp.stack([extended[:, :, 0], extended[:, :, columns + 1]], 2)
    spill_edges = with_halo(spill_edges.astype(jnp.bfloat16), (("seq", 2),), 1).astype(
        spill_edges.dtype
    )
    interior = extended[:, :, 1 : columns + 1]
    interior = interior.at[:, :, 0].add(spill_edges[:, :, 0])
    interior = interior.at[:, :, columns - 1].add(spill_edges[:, :, 3])
    carried = from_behind(interior[frames:].astype(jnp.bfloat16), "tile", 1).astype(jnp.float32)
    convolved = interior[:frames].at[:2].add(carried)
    convolved = convolved + conv_shift
    partial_value = jnp.dot(
        convolved.reshape(-1, share_width), head_weight, precision=lax.Precision.HIGHEST
    )
    summed = lax.psum(partial_value, "cfg")
    latent = (summed + mean_bias).astype(jnp.bfloat16)
    latent_dim = latent.shape[-1]
    latent = latent.reshape(frames, height // 2, 2, columns // 2, 2, latent_dim)
    patches = latent.transpose(0, 1, 3, 5, 2, 4).reshape(
        frames * (height // 2), columns // 2 * 4 * latent_dim
    )
    row_width = patches.shape[1]
    seq_count = lax.axis_size("seq")
    tile_count = lax.axis_size("tile")
    gathered = lax.all_gather(patches, "tile", axis=0, tiled=True)
    grouped = gathered.reshape(seq_count, tile_count, -1, row_width)
    own_part = lax.dynamic_index_in_dim(grouped, lax.axis_index("tile"), 1, keepdims=False)
    arrived = lax.all_to_all(own_part, "seq", split_axis=0, concat_axis=0, tiled=True)
    arrived = arrived.reshape(seq_count, -1, columns // 2, 4 * latent_dim)
    latent_tokens = arrived.transpose(1, 0, 2, 3).reshape(-1, 4 * latent_dim)
    split_at = 4 * latent_dim
    main_part = jnp.dot(noisy_tokens, patch_weight, preferred_element_type=jnp.float32) + patch_bias
    context_part = jnp.dot(
        latent_tokens, context_weight[:split_at], preferred_element_type=jnp.float32
    )
    context_part = (
        context_part
        + jnp.dot(mask_tokens, context_weight[split_at:], preferred_element_type=jnp.float32)
        + context_bias
    )
    combined = main_part + context_part
    centred = combined - jnp.mean(combined, axis=-1, keepdims=True)
    variance = jnp.mean(centred * centred, axis=-1, keepdims=True)
    return (centred * lax.rsqrt(variance + 1e-06) * (1.0 + norm_scale) + norm_shift).astype(
        jnp.bfloat16
    )


def solution(mesh):
    placed = (
        P("tile", None, "seq", None),
        P(),
        P(),
        P(),
        P(),
        P(),
        P(("seq", "tile"), None),
        P(("seq", "tile"), None),
        P(),
        P(),
        P(),
        P(),
        P(),
        P(),
    )
    return jax.shard_map(
        body, mesh=mesh, in_specs=placed, out_specs=P(("seq", "tile"), None), check_vma=False
    )
```

profile of v0, /device:TPU:0, one launch (start us, length us, event | category | flops | bytes accessed | tf_op | source)
XLA Modules:
  0.0 104.0 jit_solution(1439479919580149366)
XLA Ops:
  6.5 1.9 %fusion = f32[2,128,8]{2,1,0:T(8,128)S(1)} fusion(bf16[2,128,8,384]{3,2,1,0:T(8,128)(2,1)} %param.22), kind=kLoop, calls=%fused_computation.5 | loop fusion | flops 2357248 | bytes 1581056 | tf_op jit(solution)/shard_map/reduce_sum | solution.py:46
  8.4 0.1 copy.140
  8.5 0.1 copy.141
  8.7 2.4 %fusion.8 = bf16[2,128,8,384,1]{3,2,1,0,4:T(8,128)(2,1)S(1)} fusion(bf16[2,128,8,384]{3,2,1,0:T(8,128)(2,1)} %param.22, f32[384]{0:T(512)} %param.23, f32[2,128,8]{2,1,0:T(8,128)S(1)} %copy.141), kind=kLoop, calls=%fused_computation.13 | loop fusion | flops 6291456 | bytes 3155456 | tf_op jit(solution)/shard_map/convert_element_type | solution.py:47
  11.1 1.3 %fusion.9 = f32[2,128,8,27,16]{1,3,4,2,0:T(8,128)S(1)} fusion(bf16[2,128,8,384,1]{3,2,1,0,4:T(8,128)(2,1)S(1)} %fusion.8, bf16[27,16,384,1,1]{2,1,0,4,3:T(8,128)(2,1)S(1)} %dynamic-slice_bitcast_fusion), kind=kOutput, calls=%fused_computation.14 | convolution fusion | flops 679477248 | bytes 5443584 | tf_op jit(solution)/shard_map/dot_general | solution.py:56
  12.4 2.1 %fusion.22 = (f32[2,128,8,1,16]{1,3,4,2,0:T(1,128)S(1)}, f32[2,128,8,1,16]{1,3,4,2,0:T(1,128)S(1)}, f32[2,128,8,1,16]{1,3,4,2,0:T(1,128)S(1)}, f32[2,128,8,1,16]...) fusion(f32[2,128,8,27,16]{1,3,4,2,0:T(8,128)S(1)} %fusion.9), kind=kLoop, calls=%fused_computation.42 | loop fusion | bytes 4980736 | tf_op jit(solution)/shard_map/slice | solution.py:71
  14.5 0.0 copy-start.11
  14.5 0.0 copy-start.9
  14.5 1.0 fusion.23
  15.5 0.0 copy-start.2
  15.6 0.0 copy-start.4
  15.6 1.3 %fusion.21 = (bf16[4,130,10,16]{1,3,2,0:T(8,128)(2,1)S(1)}, f32[4,130,10,16]{1,3,2,0:T(8,128)S(1)}) fusion(f32[2,128,8,16]{1,3,2,0:T(8,128)S(1)} %bitcast.136, f32[2,128,8,16]{1,3,2,0:T(8,128)S(1)} %bitcast.137, f32[2,128,8,16]{1,3,2,0:T(8,128)S(1)} %bitcast.112, f32[2,128,8,16]{1,3,2,0:T(8,128)S(1)} %bitcast.113, f32[2,128,8,16]{1,3,2,0:T(8,128)S(1)} %bitcast.114, ...), kind=kLoop, calls=%fused_computation.41 | loop fusion | flops 2246400 | bytes 4038144 | tf_op jit(solution)/shard_map/convert.3
  16.9 0.1 fusion.24
  17.0 4.9 %collective-permute-start = (bf16[4,128,1,16]{1,3,2,0:T(8,128)(2,1)S(1)}, bf16[4,128,1,16]{1,3,2,0:T(8,128)(2,1)S(1)}, u32[]{:S(2)}, u32[]{:S(2)}) collective-permute-start(bf16[4,128,1,16]{1,3,2,0:T(8,128)(2,1)S(1)} %get-tuple-element.78), channel_id=1, source_target_pairs={{0,2},{2,4},{4,6},{6,8},{8,10},{10,12},{12,14},{1,3},{3,5},{5,7},{... | collective-permute-start | bytes 49160 | tf_op jit(solution)/shard_map/ppermute | solution.py:16
  21.8 1.3 %collective-permute-start.1 = (bf16[4,128,1,16]{1,3,2,0:T(8,128)(2,1)S(1)}, bf16[4,128,1,16]{1,3,2,0:T(8,128)(2,1)S(1)}, u32[]{:S(2)}, u32[]{:S(2)}) collective-permute-start(bf16[4,128,1,16]{1,3,2,0:T(8,128)(2,1)S(1)} %get-tuple-element.79), channel_id=1, source_target_pairs={{2,0},{4,2},{6,4},{8,6},{10,8},{12,10},{14,12},{3,1},{5,3},{7,5},{... | collective-permute-start | bytes 49160 | tf_op jit(solution)/shard_map/ppermute | solution.py:17
  23.1 0.1 slice.261
  23.3 4.2 %collective-permute-done.1 = bf16[4,128,1,16]{1,3,2,0:T(8,128)(2,1)S(1)} collective-permute-done((bf16[4,128,1,16]{1,3,2,0:T(8,128)(2,1)S(1)}, bf16[4,128,1,16]{1,3,2,0:T(8,128)(2,1)S(1)}, u32[]{:S(2)}, u32[]{:S(2)}) %collective-permute-start.1) | collective-permute-done | bytes 16416 | tf_op jit(solution)/shard_map/ppermute | solution.py:17
  27.5 0.1 fusion.17
  27.6 3.4 %collective-permute-start.2 = (bf16[2,128,8,16]{1,3,2,0:T(8,128)(2,1)S(1)}, bf16[2,128,8,16]{1,3,2,0:T(8,128)(2,1)S(1)}, u32[]{:S(2)}, u32[]{:S(2)}) collective-permute-start(bf16[2,128,8,16]{1,3,2,0:T(8,128)(2,1)S(1)} %slice.280), channel_id=1, source_target_pairs={{0,1},{2,3},{4,5},{6,7},{8,9},{10,11},{12,13},{14,15},{16,17},{18,... | collective-permute-start | bytes 196616 | tf_op jit(solution)/shard_map/ppermute | solution.py:25
  31.0 0.1 dynamic_slice.14
  31.1 1.8 %collective-permute-done.2 = bf16[2,128,8,16]{1,3,2,0:T(8,128)(2,1)S(1)} collective-permute-done((bf16[2,128,8,16]{1,3,2,0:T(8,128)(2,1)S(1)}, bf16[2,128,8,16]{1,3,2,0:T(8,128)(2,1)S(1)}, u32[]{:S(2)}, u32[]{:S(2)}) %collective-permute-start.2) | collective-permute-done | bytes 65568 | tf_op jit(solution)/shard_map/ppermute | solution.py:25
  32.9 0.1 fusion.15
  33.0 0.4 copy.170
  33.4 1.7 %fusion.18 = f32[2048,16]{0,1:T(8,128)} fusion(f32[2048,16]{1,0:T(8,128)S(1)} %bitcast.108, f32[32,16]{0,1:T(8,128)S(1)} %copy-done.9, s32[]{:T(128)S(6)} %select_n.9), kind=kOutput, calls=%fused_computation.35 | convolution fusion | flops 6291456 | bytes 264196 | tf_op jit(solution)/shard_map/dot_general | solution.py:83
  35.1 0.0 all-reduce.29.cloned.1.call-update
  35.1 0.0 copy-start.10
  35.1 0.0 copy-start.8
  35.2 5.5 %fusion.26 = f32[512,5120]{1,0:T(8,128)} fusion(bf16[512,64]{0,1:T(8,128)(2,1)S(1)} %copy-done.4, bf16[64,5120]{1,0:T(8,128)(2,1)S(1)} %copy-done.2), kind=kOutput, calls=%fused_computation.46 | convolution fusion | flops 335544320 | bytes 11206656 | tf_op jit(solution)/shard_map/dot_general | solution.py:103
  40.7 14.5 %all-reduce.29.cloned.1.call-done = f32[2048,16]{0,1:T(8,128)} async-done(((f32[2048,16]{0,1:T(8,128)}), f32[2048,16]{0,1:T(8,128)}) %all-reduce.29.cloned.1.call-update) | async-done | bytes 131088 | tf_op jit(solution)/shard_map/psum | solution.py:86
  55.2 1.0 add_convert_fusion.1
  56.2 0.3 copy.171
  56.5 0.6 copy.172
  57.0 0.1 reshape.165
  57.2 5.0 %all_gather.3 = bf16[256,256]{0,1:T(8,128)(2,1)S(1)} all-gather(bf16[128,256]{0,1:T(8,128)(2,1)S(1)} %reshape.165), channel_id=1, replica_groups=mesh['cfg'=2,'seq'=8,'tile'=2] {'tile'}, dimensions={0}, use_global_device_ids=true | all-gather | bytes 196608 | tf_op jit(solution)/shard_map/all_gather | solution.py:96
  62.2 0.1 copy.173
  62.3 0.6 dynamic-slice_bitcast_fusion.1
  62.9 5.8 %all-to-all-start = ((bf16[8,16,256]{2,1,0:T(8,128)(2,1)}), bf16[8,16,256]{2,1,0:T(8,128)(2,1)S(1)}, u32[]{:S(2)}, u32[]{:S(2)}) async-start(bf16[8,16,256]{2,1,0:T(8,128)(2,1)} %dynamic-slice_bitcast_fusion.1), calls=%async_computation | async-start | bytes 131072 | tf_op jit(solution)/shard_map/all_to_all | solution.py:99
  68.7 6.9 %all-to-all-done = bf16[8,16,256]{2,1,0:T(8,128)(2,1)S(1)} async-done(((bf16[8,16,256]{2,1,0:T(8,128)(2,1)}), bf16[8,16,256]{2,1,0:T(8,128)(2,1)S(1)}, u32[]{:S(2)}, u32[]{:S(2)}) %all-to-all-start) | async-done | bytes 65568 | tf_op jit(solution)/shard_map/all_to_all | solution.py:99
  75.6 0.1 reshape.167
  75.8 0.0 copy-start.1
  75.8 0.0 copy-start.3
  75.8 0.0 copy-start.5
  75.8 0.0 copy-start.6
  75.8 6.6 %fusion.12 = f32[512,5120]{1,0:T(8,128)} fusion(bf16[512,64]{1,0:T(8,128)(2,1)S(1)} %bitcast.110, bf16[192,5120]{1,0:T(8,128)(2,1)} %param.32), kind=kOutput, calls=%fused_computation.17 | convolution fusion | flops 335544320 | bytes 11206656 | tf_op jit(solution)/shard_map/dot_general | solution.py:104
  82.4 8.4 %fusion.25 = (f32[512]{0:T(512)S(1)}, f32[512,5120]{1,0:T(8,128)S(1)}) fusion(f32[5120]{0:T(1024)S(1)} %copy-done.5, f32[512,5120]{1,0:T(8,128)} %fusion.12, bf16[512,128]{1,0:T(8,128)(2,1)S(1)} %copy-done.3, bf16[192,5120]{1,0:T(8,128)(2,1)S(1)} %copy-done.1, f32[512,5120]{1,0:T(8,128)} %fusion.26, f32[5120]{0:T(1024)S(1)} %copy-done.6), kind=kOutput, calls=%fused_computation.45 | convolution fusion | flops 684195328 | bytes 32942080 | tf_op jit(solution)/shard_map/dot_general | solution.py:109
  90.9 0.0 copy-start.7
  90.9 1.2 %multiply_reduce_fusion = f32[512]{0:T(512)S(1)} fusion(f32[512,5120]{1,0:T(8,128)S(1)} %get-tuple-element.81, f32[512]{0:T(512)S(1)} %broadcast_multiply_fusion), kind=kLoop, calls=%fused_computation.1 | loop fusion | flops 7863808 | bytes 10489856 | tf_op jit(solution)/shard_map/reduce_sum | solution.py:114
  92.1 5.1 %add_convert_fusion = bf16[512,5120]{1,0:T(8,128)(2,1)} fusion(f32[512,5120]{1,0:T(8,128)S(1)} %get-tuple-element.81, f32[5120]{0:T(1024)S(1)} %copy-done.7, f32[5120]{0:T(1024)S(1)} %broadcast_add_fusion, f32[512]{0:T(512)S(1)} %add_rsqrt_fusion.1, f32[512]{0:T(512)S(1)} %broadcast_multiply_fusion), kind=kLoop, calls=%fused_computation | loop fusion | flops 13107200 | bytes 15773696 | tf_op jit(solution)/shard_map/convert_element_type | solution.py:115
  (23 shorter events, 0.2 us)
Async XLA Ops:
  6.5 2.1 %copy-start = (bf16[384,864]{0,1:T(8,128)(2,1)S(1)}, bf16[384,864]{0,1:T(8,128)(2,1)}, u32[]{:S(2)}) copy-start(bf16[384,864]{0,1:T(8,128)(2,1)} %param.24) | copy-start | bytes 1990660
  6.5 48.7 %all-reduce.29.cloned.1.call-start = ((), (), s32[]{:S(2)}) async-start(), calls=%async_computation.1 | async-start | bytes 262144 | tf_op jit(solution)/shard_map/psum | solution.py:86
  14.5 16.5 %copy-start.11 = (f32[32]{0:T(128)S(1)}, f32[32]{0:T(128)}, u32[]{:S(2)}) copy-start(f32[32]{0:T(128)} %param.25) | copy-start | bytes 388
  14.5 18.9 %copy-start.9 = (f32[32,16]{0,1:T(8,128)S(1)}, f32[32,16]{0,1:T(8,128)}, u32[]{:S(2)}) copy-start(f32[32,16]{0,1:T(8,128)} %param.26) | copy-start | bytes 6148
  15.5 19.6 %copy-start.2 = (bf16[64,5120]{1,0:T(8,128)(2,1)S(1)}, bf16[64,5120]{1,0:T(8,128)(2,1)}, u32[]{:S(2)}) copy-start(bf16[64,5120]{1,0:T(8,128)(2,1)} %param.30) | copy-start | bytes 1966084
  15.6 19.6 %copy-start.4 = (bf16[512,64]{0,1:T(8,128)(2,1)S(1)}, bf16[512,64]{0,1:T(8,128)(2,1)}, u32[]{:S(2)}) copy-start(bf16[512,64]{0,1:T(8,128)(2,1)} %param.28) | copy-start | bytes 196612
  17.0 6.3 %collective-permute-start = (bf16[4,128,1,16]{1,3,2,0:T(8,128)(2,1)S(1)}, bf16[4,128,1,16]{1,3,2,0:T(8,128)(2,1)S(1)}, u32[]{:S(2)}, u32[]{:S(2)}) collective-permute-start(bf16[4,128,1,16]{1,3,2,0:T(8,128)(2,1)S(1)} %get-tuple-element.78), channel_id=1, source_target_pairs={{0,2},{2,4},{4,6},{6,8},{8,10},{10,12},{12,14},{1,3},{3,5},{5,7},{... | collective-permute-start | bytes 49160 | tf_op jit(solution)/shard_map/ppermute | solution.py:16
  21.8 5.6 %collective-permute-start.1 = (bf16[4,128,1,16]{1,3,2,0:T(8,128)(2,1)S(1)}, bf16[4,128,1,16]{1,3,2,0:T(8,128)(2,1)S(1)}, u32[]{:S(2)}, u32[]{:S(2)}) collective-permute-start(bf16[4,128,1,16]{1,3,2,0:T(8,128)(2,1)S(1)} %get-tuple-element.79), channel_id=1, source_target_pairs={{2,0},{4,2},{6,4},{8,6},{10,8},{12,10},{14,12},{3,1},{5,3},{7,5},{... | collective-permute-start | bytes 49160 | tf_op jit(solution)/shard_map/ppermute | solution.py:17
  27.6 5.3 %collective-permute-start.2 = (bf16[2,128,8,16]{1,3,2,0:T(8,128)(2,1)S(1)}, bf16[2,128,8,16]{1,3,2,0:T(8,128)(2,1)S(1)}, u32[]{:S(2)}, u32[]{:S(2)}) collective-permute-start(bf16[2,128,8,16]{1,3,2,0:T(8,128)(2,1)S(1)} %slice.280), channel_id=1, source_target_pairs={{0,1},{2,3},{4,5},{6,7},{8,9},{10,11},{12,13},{14,15},{16,17},{18,... | collective-permute-start | bytes 196616 | tf_op jit(solution)/shard_map/ppermute | solution.py:25
  35.1 20.1 %copy-start.10 = (f32[16]{0:T(128)S(1)}, f32[16]{0:T(128)}, u32[]{:S(2)}) copy-start(f32[16]{0:T(128)} %param.27) | copy-start | bytes 196
  35.1 33.6 %copy-start.8 = (f32[5120]{0:T(1024)S(1)}, f32[5120]{0:T(1024)}, u32[]{:S(2)}) copy-start(f32[5120]{0:T(1024)} %param.35) | copy-start | bytes 61444
  62.9 12.7 %all-to-all-start = ((bf16[8,16,256]{2,1,0:T(8,128)(2,1)}), bf16[8,16,256]{2,1,0:T(8,128)(2,1)S(1)}, u32[]{:S(2)}, u32[]{:S(2)}) async-start(bf16[8,16,256]{2,1,0:T(8,128)(2,1)} %dynamic-slice_bitcast_fusion.1), calls=%async_computation | async-start | bytes 131072 | tf_op jit(solution)/shard_map/all_to_all | solution.py:99
  75.8 6.6 %copy-start.1 = (bf16[192,5120]{1,0:T(8,128)(2,1)S(1)}, bf16[192,5120]{1,0:T(8,128)(2,1)}, u32[]{:S(2)}) copy-start(bf16[192,5120]{1,0:T(8,128)(2,1)} %param.32) | copy-start | bytes 5898244
  75.8 6.6 %copy-start.3 = (bf16[512,128]{1,0:T(8,128)(2,1)S(1)}, bf16[512,128]{1,0:T(8,128)(2,1)}, u32[]{:S(2)}) copy-start(bf16[512,128]{1,0:T(8,128)(2,1)} %param.29) | copy-start | bytes 393220
  75.8 6.6 %copy-start.5 = (f32[5120]{0:T(1024)S(1)}, f32[5120]{0:T(1024)}, u32[]{:S(2)}) copy-start(f32[5120]{0:T(1024)} %param.33) | copy-start | bytes 61444
  75.8 6.6 %copy-start.6 = (f32[5120]{0:T(1024)S(1)}, f32[5120]{0:T(1024)}, u32[]{:S(2)}) copy-start(f32[5120]{0:T(1024)} %param.31) | copy-start | bytes 61444
  90.9 1.2 %copy-start.7 = (f32[5120]{0:T(1024)S(1)}, f32[5120]{0:T(1024)}, u32[]{:S(2)}) copy-start(f32[5120]{0:T(1024)} %param.34) | copy-start | bytes 61444
Sparse Core Ops, SparseCore 0:
  35.2 19.9 all-reduce.28
where the time goes:
time: 104 us
  waiting for transfers between devices  27.4 us (26%)
  matrix products  23.5 us (23%)
  starting transfers between devices  15.4 us (15%)
  between operations  13.7 us (13%)
  other arithmetic  12.9 us (12%)
  local copies, waits for them, and re-layouts  6.03 us (6%)
  blocking collectives  5.01 us (5%)
    psum x1, waiting for transfers between devices, body(): summed = lax.psum(partial_value, 'cfg')  14.5 us
    dot_general x1, matrix products, body(): jnp.dot(mask_tokens, context_weight[split_at:], preferred_element_type=jn...  8.42 us
    all_to_all x1, waiting for transfers between devices, body(): lax.all_to_all(own_part, 'seq', split_axis=0, concat_axis=0, tiled=True)  6.89 us
    dot_general x1, matrix products, body(): jnp.dot(latent_tokens, context_weight[:split_at], preferred_element_type=...  6.55 us
    all_to_all x1, starting transfers between devices, body(): lax.all_to_all(own_part, 'seq', split_axis=0, concat_axis=0, tiled=True)  5.78 us
    dot_general x1, matrix products, body(): jnp.dot(noisy_tokens, patch_weight, preferred_element_type=jnp.float32)  5.52 us
    convert_element_type x1, other arithmetic, body(): (centred * lax.rsqrt(variance + 1e-06) * (1.0 + norm_scale) + norm_shift)...  5.05 us
    all_gather x1, blocking collectives, body(): gathered = lax.all_gather(patches, 'tile', axis=0, tiled=True)  5.01 us
  transfers between devices with their start and end apart: 5, of which 4 were waited for; matrix products, arithmetic and copies ran while one was open for 6% of the time, Pallas kernels for 0%

commit v1 on v0

v1 whole, which is shorter than its diff:
```python
import functools

import jax
import jax.numpy as jnp
from jax import lax
from jax.experimental import pallas as pl
from jax.experimental.pallas import tpu as pltpu
from jax.sharding import PartitionSpec as P

K = 3
MESH = pl.DeviceIdType.MESH
F32 = jnp.float32
BF16 = jnp.bfloat16


def fold_weights(conv_weight, mean_weight):
    zo, z = mean_weight.shape
    taps = K * K * K
    width = 2 * K * 4 * 4 * z
    row = lax.broadcasted_iota(jnp.int32, (taps, zo, width), 0)
    col = lax.broadcasted_iota(jnp.int32, (taps, zo, width), 2)
    a, b, e = row // (K * K), row // K % K, row % K
    group = col // z
    g, slot, b_out, frame = group % 4, group // 4 % 4, group // 16 % K, group // (16 * K)
    e_out = jnp.where(slot == 0, 1, jnp.where(slot == 1, -1, jnp.where(slot == 2, 0, 2)))
    keep = (b == b_out) & (e == e_out) & (a == frame + 2 - g)
    high = mean_weight.astype(BF16)
    low = (mean_weight - high.astype(F32)).astype(BF16)
    copier = (
        lax.broadcasted_iota(jnp.int32, (z, width), 0)
        == lax.broadcasted_iota(jnp.int32, (z, width), 1) % z
    ).astype(BF16)
    total = None
    for part in (high, low):
        wide = jnp.dot(part, copier, preferred_element_type=F32).astype(BF16)
        mat = jnp.where(keep, wide[None], jnp.zeros((), BF16)).reshape(taps * zo, width)
        term = jnp.dot(conv_weight, mat, preferred_element_type=F32)
        total = term if total is None else total + term
    return total.astype(BF16)


def head_kernel(
    sizes, x_hbm, w_ref, gain_ref, bias_ref, out_ref,
    xin, actf, acc, edge, pk, rs_send, ls_send, ca_send, rs_got, ls_got, ca_got, patch,
    in_sem, s1_sem, r1_sem, s2_sem, r2_sem,
):
    n_c, n_s, n_t, shard_rows = sizes
    c, s, t = lax.axis_index("cfg"), lax.axis_index("seq"), lax.axis_index("tile")
    frames, height, columns, channels = x_hbm.shape
    half = height // n_c
    pairs = half // 2
    z = 16
    chunks = pairs // shard_rows
    chunk_tokens = shard_rows * (columns // 2)

    def dev(ci, si, ti):
        return {"cfg": ci, "seq": si, "tile": ti}

    load = pltpu.make_async_copy(
        x_hbm.at[:, pl.ds(c * (half - 1), half + 1)],
        xin.at[:, pl.ds(1 - c, half + 1)],
        in_sem,
    )
    load.start()

    barrier = pltpu.get_barrier_semaphore()
    links = [(1, 0), (-1, 0), (0, 1), (1, 1), (-1, 1)]

    def there(ds, dt, sign):
        si, ti = s + sign * ds, t + sign * dt
        return (si >= 0) & (si < n_s) & (ti >= 0) & (ti < n_t), si, ti

    expect = jnp.int32(0)
    for ds, dt in links:
        ok, si, ti = there(ds, dt, -1)

        @pl.when(ok)
        def _():
            pl.semaphore_signal(barrier, inc=1, device_id=dev(c, si, ti), device_id_type=MESH)

        ok, _, _ = there(ds, dt, 1)
        expect = expect + ok.astype(jnp.int32)

    first = (s * n_t + t) * shard_rows
    src_t = first // (height // 2) // frames
    src_c = first % (height // 2) // pairs
    for si in range(n_s):
        mine = (src_c == c) & (src_t == t) & (s == si)

        @pl.when(jnp.logical_not(mine))
        def _():
            pl.semaphore_signal(barrier, inc=1, device_id=dev(src_c, si, src_t), device_id_type=MESH)

    own = (src_c == c) & (src_t == t)
    expect = expect + frames * chunks * n_c - own.astype(jnp.int32)

    zero_row = jnp.zeros((frames, 1, columns, channels), BF16)

    @pl.when(c == 0)
    def _():
        xin[:, 0:1] = zero_row

    @pl.when(c == n_c - 1)
    def _():
        xin[:, half + 1 : half + 2] = zero_row

    load.wait()
    gain = gain_ref[...]
    step_rows = 6 if (half + 2) % 6 == 0 else 2
    for f in range(frames):

        @pl.loop(0, (half + 2) // step_rows)
        def _(r):
            v = xin[f, pl.ds(r * step_rows, step_rows)].astype(F32)
            v = v.reshape(step_rows * columns, channels)
            energy = jnp.sum(v * v, axis=-1, keepdims=True) * (1.0 / channels)
            v = v * lax.rsqrt(energy + 1e-06) * gain
            v = v / (1.0 + jnp.exp(-v))
            at = pl.multiple_of(r * (step_rows * columns), step_rows * columns)
            actf[f, pl.ds(at, step_rows * columns), :] = v

    rows = half * columns
    for m in range(4):
        lo = m * (rows // 4)
        total = None
        for f in range(frames):
            for b in range(K):
                lhs = actf[f, lo + b * columns : lo + b * columns + rows // 4, :].astype(BF16)
                k = (f * K + b) * 256
                term = jnp.dot(lhs, w_ref[:, k : k + 256], preferred_element_type=F32)
                total = term if total is None else total + term
        acc[lo : lo + rows // 4, :] = total[:, :128]
        edge[lo : lo + rows // 4, :] = total[:, 128:]

    q = edge[...]
    w_at = lax.broadcasted_iota(jnp.int32, (rows, 128), 0) % columns
    right = jnp.where(w_at == 0, 0.0, pltpu.roll(q, 1, 0))
    left = jnp.where(w_at == columns - 1, 0.0, pltpu.roll(q, rows - 1, 0))
    acc[...] = acc[...] + right + pltpu.roll(left, 64, 1)
    rs_send[...] = edge[pl.ds(columns - 1, half, stride=columns), :].astype(BF16)
    ls_send[...] = edge[pl.ds(0, half, stride=columns), :].astype(BF16)
    quarter = rows // 4
    lane = lax.broadcasted_iota(jnp.int32, (quarter, 128), 1)
    packed = jnp.zeros((quarter, 128), F32)
    for k in range(4):
        part = pltpu.roll(acc[k * quarter : (k + 1) * quarter, :], (k * 32 + 128 - 32) % 128, 1)
        packed = jnp.where(lane // 32 == k, part, packed)
    ca_send[...] = packed.astype(BF16)

    pl.semaphore_wait(barrier, expect)

    bufs = {1: (rs_send, rs_got), -1: (ls_send, ls_got), 0: (ca_send, ca_got)}

    def link_copy(i, sign):
        ds, dt = links[i]
        ok, si, ti = there(ds, dt, sign)
        src, dst = bufs[ds]
        if ds != 0:
            dst = dst.at[dt]
        return ok, pltpu.make_async_remote_copy(
            src_ref=src, dst_ref=dst, send_sem=s1_sem.at[i], recv_sem=r1_sem.at[i],
            device_id=dev(c, si, ti), device_id_type=MESH,
        )

    for i in (2, 3, 4, 0, 1):
        ok, copy = link_copy(i, 1)

        @pl.when(ok)
        def _():
            copy.start()

    for i in (0, 1, 3, 4, 2):
        ds, dt = links[i]
        ok, copy = link_copy(i, -1)

        @pl.when(ok)
        def _():
            copy.wait_recv()
            if ds == 0:
                got = ca_got[...].astype(F32)
                for k in range(4):
                    acc[k * quarter : (k + 1) * quarter, :] += pltpu.roll(got, (128 - 32 * k) % 128, 1)
            else:
                got = bufs[ds][1][dt].astype(F32)
                turn = (128 - 32 * dt - (64 if ds < 0 else 0)) % 128
                if turn:
                    got = pltpu.roll(got, turn, 1)
                at = pl.ds(0 if ds > 0 else columns - 1, half, stride=columns)
                acc[at, :] = acc[at, :] + got

    total = acc[...] + bias_ref[...]
    by_row = total.reshape(pairs, 2, columns, 128)
    even = by_row[:, 0].reshape(pairs * columns, 128)
    odd = by_row[:, 1].reshape(pairs * columns, 128)
    lane = lax.broadcasted_iota(jnp.int32, (pairs * columns, 128), 1)
    mixed = jnp.where(
        lane < 16, even,
        jnp.where(
            lane < 32, pltpu.roll(odd, 16, 1),
            jnp.where(lane < 48, pltpu.roll(even, 16, 1), pltpu.roll(odd, 32, 1)),
        ),
    )
    pk[...] = mixed
    tokens = pairs * columns // 2
    left_half = pk[pl.ds(0, tokens, stride=2), :]
    right_half = pk[pl.ds(1, tokens, stride=2), :]
    lane = lax.broadcasted_iota(jnp.int32, (tokens, 128), 1)
    for f in range(frames):
        one = left_half if f == 0 else pltpu.roll(left_half, 128 - 32 * f, 1)
        two = pltpu.roll(right_half, (32 - 32 * f) % 128, 1) if f != 1 else right_half
        both = jnp.where(lane < 32, one, two)
        for m in range(chunks):
            patch[f * chunks + m] = both[m * chunk_tokens : (m + 1) * chunk_tokens, :64].astype(BF16)

    def patch_copy(f, m, ci):
        shard = ((t * frames + f) * (height // 2) + c * pairs) // shard_rows + m
        si, ti = shard // n_t, shard % n_t
        mine = (si == s) & (ti == t) & (c == ci)
        piece = f * chunks + m
        local = pltpu.make_async_copy(patch.at[piece], out_ref.at[s], r2_sem.at[s])
        away = pltpu.make_async_remote_copy(
            src_ref=patch.at[piece], dst_ref=out_ref.at[s],
            send_sem=s2_sem.at[piece * n_c + ci], recv_sem=r2_sem.at[s],
            device_id=dev(ci, si, ti), device_id_type=MESH,
        )
        return mine, local, away

    every = [(f, m, ci) for f in range(frames) for m in range(chunks) for ci in range(n_c)]
    for item in every:
        mine, local, away = patch_copy(*item)

        @pl.when(mine)
        def _():
            local.start()

        @pl.when(jnp.logical_not(mine))
        def _():
            away.start()

    for si in range(n_s):
        pltpu.make_async_copy(patch.at[0], out_ref.at[si], r2_sem.at[si]).wait()
    for i in range(5):
        ok, copy = link_copy(i, 1)

        @pl.when(ok)
        def _():
            copy.wait_send()

    for item in every:
        mine, _, away = patch_copy(*item)

        @pl.when(jnp.logical_not(mine))
        def _():
            away.wait_send()


def tail_kernel(noisy, mask, lat, pw, cw, pb, cb, shift, scale, out, comb):
    split = lat.shape[1]
    width = comb.shape[1]
    step = 512
    z = split // 4
    got = lax.broadcasted_iota(jnp.int32, (split, split), 0)
    want = lax.broadcasted_iota(jnp.int32, (split, split), 1)
    perm = (want == (got % z) * 4 + (got // z % 2) * 2 + got // (2 * z)).astype(BF16)
    tokens = jnp.dot(lat[...], perm, preferred_element_type=F32).astype(BF16)
    total = None
    for k in range(0, width, step):
        at = slice(k, k + step)
        part = jnp.dot(noisy[...], pw[:, at], preferred_element_type=F32)
        part = part + jnp.dot(tokens, cw[:split, at], preferred_element_type=F32)
        part = part + jnp.dot(mask[...], cw[split:, at], preferred_element_type=F32)
        part = part + (pb[:, at] + cb[:, at])
        comb[:, at] = part
        term = jnp.sum(part, axis=-1, keepdims=True)
        total = term if total is None else total + term
    mean = total * (1.0 / width)
    square = None
    for k in range(0, width, step):
        d = comb[:, k : k + step] - mean
        term = jnp.sum(d * d, axis=-1, keepdims=True)
        square = term if square is None else square + term
    inv = lax.rsqrt(square * (1.0 / width) + 1e-06)
    for k in range(0, width, step):
        at = slice(k, k + step)
        out[:, at] = ((comb[:, at] - mean) * inv * (1.0 + scale[:, at]) + shift[:, at]).astype(BF16)


def body(
    section_input, norm_gain, conv_weight, conv_bias, mean_weight, mean_bias, noisy_tokens,
    mask_tokens, patch_weight, patch_bias, context_weight, context_bias, norm_shift, norm_scale,
):
    frames, height, columns, channels = section_input.shape
    n_c, n_s, n_t = lax.axis_size("cfg"), lax.axis_size("seq"), lax.axis_size("tile")
    z = mean_weight.shape[1]
    tokens = noisy_tokens.shape[0]
    shard_rows = tokens // (n_s * columns // 2)
    half = height // n_c
    rows = half * columns
    chunks = half // 2 // shard_rows
    chunk_tokens = shard_rows * (columns // 2)
    weight = fold_weights(conv_weight, mean_weight)
    bias = jnp.dot(conv_bias[None], mean_weight, precision=lax.Precision.HIGHEST) + mean_bias
    bias = jnp.tile(bias, (1, 128 // z))
    vmem = pl.BlockSpec(memory_space=pltpu.VMEM)
    arrived = pl.pallas_call(
        functools.partial(head_kernel, (n_c, n_s, n_t, shard_rows)),
        out_shape=jax.ShapeDtypeStruct((n_s, chunk_tokens, 4 * z), BF16),
        in_specs=[pl.BlockSpec(memory_space=pl.ANY), vmem, vmem, vmem],
        out_specs=vmem,
        scratch_shapes=[
            pltpu.VMEM((frames, half + 2, columns, channels), BF16),
            pltpu.VMEM((frames, (half + 2) * columns, channels), F32),
            pltpu.VMEM((rows, 128), F32),
            pltpu.VMEM((rows, 128), F32),
            pltpu.VMEM((rows // 2, 128), F32),
            pltpu.VMEM((half, 128), BF16),
            pltpu.VMEM((half, 128), BF16),
            pltpu.VMEM((rows // 4, 128), BF16),
            pltpu.VMEM((2, half, 128), BF16),
            pltpu.VMEM((2, half, 128), BF16),
            pltpu.VMEM((rows // 4, 128), BF16),
            pltpu.VMEM((frames * chunks, chunk_tokens, 4 * z), BF16),
            pltpu.SemaphoreType.DMA,
            pltpu.SemaphoreType.DMA((5,)),
            pltpu.SemaphoreType.DMA((5,)),
            pltpu.SemaphoreType.DMA((frames * chunks * n_c,)),
            pltpu.SemaphoreType.DMA((n_s,)),
        ],
        compiler_params=pltpu.CompilerParams(collective_id=0, has_side_effects=True),
        name="head",
    )(section_input, weight, norm_gain[None], bias)
    lat = arrived.reshape(n_s, shard_rows, columns // 2, 4 * z).transpose(1, 0, 2, 3)
    lat = lat.reshape(tokens, 4 * z)

    width = patch_weight.shape[1]
    block = min(tokens, 128)
    tok = lambda n: pl.BlockSpec((block, n), lambda i: (i, 0))
    full = lambda a: pl.BlockSpec(a.shape, lambda i: (0, 0))
    vecs = [v[None] for v in (patch_bias, context_bias, norm_shift, norm_scale)]
    return pl.pallas_call(
        tail_kernel,
        out_shape=jax.ShapeDtypeStruct((tokens, width), BF16),
        grid=(tokens // block,),
        in_specs=[tok(noisy_tokens.shape[1]), tok(mask_tokens.shape[1]), tok(4 * z)]
        + [full(a) for a in (patch_weight, context_weight)]
        + [full(v) for v in vecs],
        out_specs=tok(width),
        scratch_shapes=[pltpu.VMEM((block, width), F32)],
        name="tail",
    )(noisy_tokens, mask_tokens, lat, patch_weight, context_weight, *vecs)


def solution(mesh):
    placed = (P("tile", None, "seq", None),) + (P(),) * 5
    placed = placed + (P(("seq", "tile"), None),) * 2 + (P(),) * 6
    return jax.shard_map(
        body, mesh=mesh, in_specs=placed, out_specs=P(("seq", "tile"), None), check_vma=False
    )
```

time: 104 us -> 50.3 us (0.48)
  Pallas kernels: 0 us -> 31.2 us
  waiting for transfers between devices: 27.4 us -> 0 us
  matrix products: 23.5 us -> 5.93 us
  starting transfers between devices: 15.4 us -> 0 us
  between operations: 13.7 us -> 0.13 us
  other arithmetic: 12.9 us -> 7.84 us
  blocking collectives: 5.01 us -> 0 us
  local copies, waits for them, and re-layouts: 6.03 us -> 4.93 us
    pallas_call x0 -> x2, Pallas kernels: none -> 31.2 us  [the longest x1 19.3 us: body(): pl.pallas_call(functools.partial(head_kernel, (n_c, n_s, n_t, shard_rows)...]
    dot_general x5, matrix products: 23.5 us -> 5.93 us  [the longest x2 3.92 us: fold_weights(): term = jnp.dot(conv_weight, mat, preferred_element_type=F32)]
    psum x1 -> x0, waiting for transfers between devices: 14.5 us -> none  [body(): summed = lax.psum(partial_value, 'cfg')]
    ppermute x3 -> x0, starting transfers between devices: 9.59 us -> none  [the longest x1 4.87 us: with_halo(): before = lax.ppermute(last, axis, up)]
    convert_element_type x3 -> x0, other arithmetic: 8.41 us -> none  [the longest x1 5.05 us: body(): (centred * lax.rsqrt(variance + 1e-06) * (1.0 + norm_scale) + norm_shift)...]
    select_n x0 -> x1, other arithmetic: none -> 7.74 us  [fold_weights(): jnp.where(keep, wide[None], jnp.zeros((), BF16)).reshape(taps * zo, width)]
    all_to_all x1 -> x0, waiting for transfers between devices: 6.89 us -> none  [body(): lax.all_to_all(own_part, 'seq', split_axis=0, concat_axis=0, tiled=True)]
    ppermute x3 -> x0, waiting for transfers between devices: 5.99 us -> none  [the longest x1 4.19 us: with_halo(): after = lax.ppermute(first, axis, down)]
  transfers between devices with their start and end apart: 5 -> 0, of which waited for: 4 -> 0; matrix products, arithmetic and copies ran while one was open for 6% -> 0% of each run, Pallas kernels for 0% -> 0%
where the time goes in v1:
time: 50.3 us; the launch traced here: 50 us
  Pallas kernels  31.2 us (62%)
  other arithmetic  7.84 us (16%)
  matrix products  5.93 us (12%)
  local copies, waits for them, and re-layouts  4.93 us (10%)
    pallas_call x1, Pallas kernels, body(): pl.pallas_call(functools.partial(head_kernel, (n_c, n_s, n_t, shard_rows)...  19.3 us
    pallas_call x1, Pallas kernels, body(): pl.pallas_call(tail_kernel, out_shape=jax.ShapeDtypeStruct((tokens, width...  11.9 us
    select_n x1, other arithmetic, fold_weights(): jnp.where(keep, wide[None], jnp.zeros((), BF16)).reshape(taps * zo, width)  7.74 us
    dot_general x2, matrix products, fold_weights(): term = jnp.dot(conv_weight, mat, preferred_element_type=F32)  3.92 us
    dot_general x2, matrix products, fold_weights(): wide = jnp.dot(part, copier, preferred_element_type=F32).astype(BF16)  1.88 us
    reshape x1, local copies, waits for them, and re-layouts, body(): arrived.reshape(n_s, shard_rows, columns // 2, 4 * z).transpose(1, 0, 2, 3)  1.61 us
    iota x15, local copies, waits for them, and re-layouts, fold_weights(): row = lax.broadcasted_iota(jnp.int32, (taps, zo, width), 0)  1.1 us

profile of v1, /device:TPU:0, one launch (start us, length us, event | category | flops | bytes accessed | tf_op | source)
XLA Modules:
  0.0 50.0 jit_solution(15731662399279603005)
XLA Ops:
  0.0 0.0 copy-start
  0.0 1.0 %convolution_convert_fusion = bf16[32,1536]{1,0:T(8,128)(2,1)S(1)} fusion(s32[1536]{0:T(1024)S(1)} %get-tuple-element.7, s32[1536]{0:T(1024)S(1)} %get-tuple-element.8, pred[1536]{0:T(1024)(128)(4,1)S(1)} %fusion.33, f32[32,16]{0,1:T(8,128)} %param.18), kind=kOutput, calls=%fused_computation.46 | convolution fusion | flops 1673216 | bytes 114176 | tf_op jit(solution)/shard_map/dot_general | solution.py:35
  1.0 0.9 %fusion.22 = bf16[32,1536]{1,0:T(8,128)(2,1)S(1)} fusion(s32[1536]{0:T(1024)S(1)} %get-tuple-element.7, s32[1536]{0:T(1024)S(1)} %get-tuple-element.8, pred[1536]{0:T(1024)(128)(4,1)S(1)} %fusion.33, f32[32,16]{0,1:T(8,128)} %param.18), kind=kOutput, calls=%fused_computation.48 | convolution fusion | flops 1671680 | bytes 114176 | tf_op jit(solution)/shard_map/dot_general | solution.py:35
  1.9 0.1 iota.148
  2.0 0.1 iota.149
  2.1 0.1 iota.151
  2.1 0.1 iota.152
  2.2 0.1 iota.160
  2.3 0.1 iota.161
  2.4 0.1 iota.163
  2.5 0.1 iota.164
  2.5 0.1 iota.168
  2.6 0.1 iota.169
  2.7 0.1 iota.171
  2.8 0.1 iota.172
  2.9 0.1 iota.146
  2.9 0.1 and.137
  3.0 0.1 iota.158
  3.1 0.1 and.143
  3.2 0.1 iota.166
  3.3 0.1 and.148
  3.4 7.7 %bitcast_select_fusion = (bf16[864,1536]{1,0:T(8,128)(2,1)S(1)}, bf16[864,1536]{1,0:T(8,128)(2,1)S(1)}) fusion(bf16[32,1536]{1,0:T(8,128)(2,1)S(1)} %convolution_convert_fusion, s32[864]{0:T(1024)S(1)} %iota.172, s32[864]{0:T(1024)S(1)} %iota.169, pred[864]{0:T(1024)(128)(4,1)S(1)} %and.148, s32[864]{0:T(1024)S(1)} %iota.164, s32[864]{0:T(1024)S(1)} %iota.161, ...), kind=kLoop, calls=%fused_computation.43 | loop fusion | flops 102187008 | bytes 5542176 | tf_op jit(solution)/shard_map/jit(_where)/select_n | solution.py:36
  11.2 0.0 copy-done
  11.2 1.5 %fusion.39 = f32[1536,384]{0,1:T(8,128)S(1)} fusion(bf16[864,1536]{1,0:T(8,128)(2,1)S(1)} %get-tuple-element.6, bf16[384,864]{0,1:T(8,128)(2,1)S(1)} %copy-done), kind=kOutput, calls=%fused_computation.83 | convolution fusion | flops 1019215872 | bytes 5677056 | tf_op jit(solution)/shard_map/dot_general | solution.py:37
  12.6 0.0 copy-start.1
  12.6 0.0 copy-start.4
  12.6 0.0 copy-start.5
  12.7 0.0 copy-start.3
  12.7 0.0 copy-start.2
  12.7 2.5 %fusion.21.w_ref = bf16[384,1536]{1,0:T(8,128)(2,1)} fusion(f32[1536,384]{0,1:T(8,128)S(1)} %fusion.39, bf16[864,1536]{1,0:T(8,128)(2,1)S(1)} %get-tuple-element.5, bf16[384,864]{0,1:T(8,128)(2,1)S(1)} %copy-done), kind=kOutput, calls=%fused_computation.45 | convolution fusion | flops 1020395520 | bytes 6856704 | tf_op jit(solution)/shard_map/dot_general | solution.py:37
  15.2 0.0 copy-done.1
  15.2 0.0 copy-done.4
  15.2 0.0 copy-done.5
  15.2 0.1 fusion.23
  15.3 0.6 %tile.10.bias_ref = f32[1,128]{1,0:T(1,128)} reshape(f32[8,16]{1,0:T(8,128)S(1)} %tile.4) | data formatting | bytes 1024 | tf_op jit(solution)/shard_map/tile | solution.py:303
  15.9 0.0 copy-done.3
  15.9 0.6 %broadcast_in_dim.53.gain_ref = f32[1,384]{1,0:T(1,128)} reshape(f32[384]{0:T(512)S(1)} %copy-done.3) | data formatting | bytes 3072 | tf_op jit(solution)/shard_map/broadcast_in_dim | solution.py:331
  16.5 19.3 %head.1 = bf16[8,64,64]{2,1,0:T(8,128)(2,1)} custom-call(bf16[2,128,8,384]{3,2,1,0:T(8,128)(2,1)} %x_hbm.1, bf16[384,1536]{1,0:T(8,128)(2,1)} %fusion.21.w_ref, f32[1,384]{1,0:T(1,128)} %broadcast_in_dim.53.gain_ref, f32[1,128]{1,0:T(1,128)} %tile.10.bias_ref), custom_call_target="tpu_custom_call" | custom-call | tf_op jit(solution)/shard_map/head/pallas_call | solution.py:305
  35.7 1.6 %copy.17 = bf16[8,16,4,64]{3,2,0,1:T(4,128)(2,1)} copy(bf16[8,16,4,64]{3,2,1,0:T(4,128)(2,1)} %bitcast.29) | data formatting | bytes 131072 | tf_op jit(solution)/shard_map/reshape | solution.py:332
  37.3 0.0 copy-done.2
  37.3 0.8 %copy.18.noisy = bf16[512,64]{1,0:T(8,128)(2,1)} copy(bf16[512,64]{0,1:T(8,128)(2,1)S(1)} %copy-done.2) | data formatting | bytes 131072 | tf_op args[6]
  38.1 11.9 %tail.1 = bf16[512,5120]{1,0:T(8,128)(2,1)} custom-call(bf16[512,64]{1,0:T(8,128)(2,1)} %copy.18.noisy, bf16[512,128]{1,0:T(8,128)(2,1)} %mask.1, bf16[512,64]{1,0:T(8,128)(2,1)} %bitcast.28, bf16[64,5120]{1,0:T(8,128)(2,1)} %pw.1, bf16[192,5120]{1,0:T(8,128)(2,1)} %cw.1, f32[1,5120]{1,0:T(1,128)} %bitcast.30, f32[1,5120]{1,0:T(1,128)} %bitcast.31, ...), custom_call_target="tpu_custom_call" | custom-call | tf_op jit(solution)/shard_map/tail/pallas_call | solution.py:340
  (14 shorter events, 0.1 us)
Async XLA Ops:
  0.0 11.2 %copy-start = (bf16[384,864]{0,1:T(8,128)(2,1)S(1)}, bf16[384,864]{0,1:T(8,128)(2,1)}, u32[]{:S(2)}) copy-start(bf16[384,864]{0,1:T(8,128)(2,1)} %param.16) | copy-start | bytes 1990660
  12.6 2.5 %copy-start.1 = (f32[32,16]{0,1:T(8,128)S(1)}, f32[32,16]{0,1:T(8,128)}, u32[]{:S(2)}) copy-start(f32[32,16]{0,1:T(8,128)} %param.18) | copy-start | bytes 6148
  12.6 2.5 %copy-start.4 = (f32[16]{0:T(128)S(1)}, f32[16]{0:T(128)}, u32[]{:S(2)}) copy-start(f32[16]{0:T(128)} %param.19) | copy-start | bytes 196
  12.6 2.5 %copy-start.5 = (f32[32]{0:T(128)S(1)}, f32[32]{0:T(128)}, u32[]{:S(2)}) copy-start(f32[32]{0:T(128)} %param.17) | copy-start | bytes 388
  12.7 3.2 %copy-start.3 = (f32[384]{0:T(512)S(1)}, f32[384]{0:T(512)}, u32[]{:S(2)}) copy-start(f32[384]{0:T(512)} %param.15) | copy-start | bytes 4612
  12.7 24.7 %copy-start.2 = (bf16[512,64]{0,1:T(8,128)(2,1)S(1)}, bf16[512,64]{0,1:T(8,128)(2,1)}, u32[]{:S(2)}) copy-start(bf16[512,64]{0,1:T(8,128)(2,1)} %param.20) | copy-start | bytes 196612

commit v2 on v1

--- a/solution.py
+++ b/solution.py
@@ -13,35 +13,63 @@
 BF16 = jnp.bfloat16
 
 
-def fold_weights(conv_weight, mean_weight):
-    zo, z = mean_weight.shape
-    taps = K * K * K
-    width = 2 * K * 4 * 4 * z
-    row = lax.broadcasted_iota(jnp.int32, (taps, zo, width), 0)
-    col = lax.broadcasted_iota(jnp.int32, (taps, zo, width), 2)
-    a, b, e = row // (K * K), row // K % K, row % K
-    group = col // z
-    g, slot, b_out, frame = group % 4, group // 4 % 4, group // 16 % K, group // (16 * K)
-    e_out = jnp.where(slot == 0, 1, jnp.where(slot == 1, -1, jnp.where(slot == 2, 0, 2)))
-    keep = (b == b_out) & (e == e_out) & (a == frame + 2 - g)
-    high = mean_weight.astype(BF16)
-    low = (mean_weight - high.astype(F32)).astype(BF16)
-    copier = (
-        lax.broadcasted_iota(jnp.int32, (z, width), 0)
-        == lax.broadcasted_iota(jnp.int32, (z, width), 1) % z
-    ).astype(BF16)
-    total = None
+def ones_where(shape, test):
+    i = lax.broadcasted_iota(jnp.int32, shape, 0)
+    j = lax.broadcasted_iota(jnp.int32, shape, 1)
+    return jnp.where(test(i, j), 1.0, 0.0)
+
+
+def nt(x, y):
+    return lax.dot_general(x, y, (((1,), (1,)), ((), ())), preferred_element_type=F32)
+
+
+def fold_weights(cw_ref, mw_ref, wt):
+    z, zo = mw_ref.shape
+    mw = mw_ref[...]
+    high = mw.astype(BF16)
+    low = (mw - high.astype(F32)).astype(BF16)
+    spread = ones_where((4 * z, z), lambda i, j: i % z == j).astype(BF16)
+    copier = ones_where((zo, K * zo), lambda i, j: j % zo == i).astype(BF16)
+
+    def right_slot(i, j):
+        slot, e = i // z, j // zo
+        return ((slot == 0) & (e == 1)) | ((slot == 2) & (e == 0)) | ((slot == 3) & (e == 2))
+
+    keep = ones_where((4 * z, K * zo), right_slot)
+    parts = []
     for part in (high, low):
-        wide = jnp.dot(part, copier, preferred_element_type=F32).astype(BF16)
-        mat = jnp.where(keep, wide[None], jnp.zeros((), BF16)).reshape(taps * zo, width)
-        term = jnp.dot(conv_weight, mat, preferred_element_type=F32)
-        total = term if total is None else total + term
-    return total.astype(BF16)
+        tall = jnp.dot(spread, part, preferred_element_type=F32).astype(BF16)
+        parts.append((jnp.dot(tall, copier, preferred_element_type=F32) * keep).astype(BF16))
+    nothing = jnp.zeros((z, wt.shape[2]), BF16)
+    for a in range(K):
+        for b in range(K):
+            at = (a * K + b) * K * zo
+            rhs = cw_ref[at : at + K * zo, :]
+            res = sum(jnp.dot(p, rhs, preferred_element_type=F32) for p in parts).astype(BF16)
+            for f in range(2):
+                for slot in range(4):
+                    row = slot * 4 * z + (f + 2 - a) * z
+                    wt[f * K + b, row : row + z, :] = res[slot * z : (slot + 1) * z]
+    for b in range(K):
+        for slot in range(4):
+            row = slot * 4 * z
+            wt[b, row + 3 * z : row + 4 * z, :] = nothing
+            wt[K + b, row : row + z, :] = nothing
+
+
+def fold_bias(mw_ref, cb_ref, mb_ref):
+    z = mw_ref.shape[0]
+    copier = ones_where((128, z), lambda i, j: i % z == j)
+    exact = functools.partial(
+        lax.dot_general, dimension_numbers=(((1,), (1,)), ((), ())),
+        precision=lax.Precision.HIGHEST, preferred_element_type=F32,
+    )
+    return exact(exact(cb_ref[...], mw_ref[...]) + mb_ref[...], copier)
 
 
 def head_kernel(
-    sizes, x_hbm, w_ref, gain_ref, bias_ref, out_ref,
-    xin, actf, acc, edge, pk, rs_send, ls_send, ca_send, rs_got, ls_got, ca_got, patch,
+    sizes, x_hbm, cw_ref, gain_ref, mw_ref, cb_ref, mb_ref, out_ref,
+    wt, xin, actf, acc, edge, pk, rs_send, ls_send, ca_send, rs_got, ls_got, ca_got, patch,
     in_sem, s1_sem, r1_sem, s2_sem, r2_sem,
 ):
     n_c, n_s, n_t, shard_rows = sizes
@@ -94,6 +122,9 @@
     own = (src_c == c) & (src_t == t)
     expect = expect + frames * chunks * n_c - own.astype(jnp.int32)
 
+    fold_weights(cw_ref, mw_ref, wt)
+    bias = fold_bias(mw_ref, cb_ref, mb_ref)
+
     zero_row = jnp.zeros((frames, 1, columns, channels), BF16)
 
     @pl.when(c == 0)
@@ -120,17 +151,16 @@
             actf[f, pl.ds(at, step_rows * columns), :] = v
 
     rows = half * columns
-    for m in range(4):
-        lo = m * (rows // 4)
+    for m in range(2):
+        lo = m * (rows // 2)
         total = None
         for f in range(frames):
             for b in range(K):
-                lhs = actf[f, lo + b * columns : lo + b * columns + rows // 4, :].astype(BF16)
-                k = (f * K + b) * 256
-                term = jnp.dot(lhs, w_ref[:, k : k + 256], preferred_element_type=F32)
+                lhs = actf[f, lo + b * columns : lo + b * columns + rows // 2, :].astype(BF16)
+                term = nt(lhs, wt[f * K + b])
                 total = term if total is None else total + term
-        acc[lo : lo + rows // 4, :] = total[:, :128]
-        edge[lo : lo + rows // 4, :] = total[:, 128:]
+        acc[lo : lo + rows // 2, :] = total[:, :128]
+        edge[lo : lo + rows // 2, :] = total[:, 128:]
 
     q = edge[...]
     w_at = lax.broadcasted_iota(jnp.int32, (rows, 128), 0) % columns
@@ -188,7 +218,7 @@
                 at = pl.ds(0 if ds > 0 else columns - 1, half, stride=columns)
                 acc[at, :] = acc[at, :] + got
 
-    total = acc[...] + bias_ref[...]
+    total = acc[...] + bias
     by_row = total.reshape(pairs, 2, columns, 128)
     even = by_row[:, 0].reshape(pairs * columns, 128)
     odd = by_row[:, 1].reshape(pairs * columns, 128)
@@ -254,21 +284,42 @@
             away.wait_send()
 
 
-def tail_kernel(noisy, mask, lat, pw, cw, pb, cb, shift, scale, out, comb):
-    split = lat.shape[1]
+def tail_kernel(noisy, mask, lat, pw, cw, pb, cb, shift, scale, out, comb, both, sems):
+    split = lat.shape[-1]
     width = comb.shape[1]
     step = 512
     z = split // 4
-    got = lax.broadcasted_iota(jnp.int32, (split, split), 0)
-    want = lax.broadcasted_iota(jnp.int32, (split, split), 1)
-    perm = (want == (got % z) * 4 + (got // z % 2) * 2 + got // (2 * z)).astype(BF16)
-    tokens = jnp.dot(lat[...], perm, preferred_element_type=F32).astype(BF16)
+
+    @pl.when(pl.program_id(0) == 0)
+    def _():
+        upper = pltpu.make_async_copy(pw, both.at[:split], sems.at[0])
+        lower = pltpu.make_async_copy(cw, both.at[split:], sems.at[1])
+        upper.start()
+        lower.start()
+        upper.wait()
+        lower.wait()
+
+    perm = ones_where(
+        (split, split), lambda i, j: j == (i % z) * 4 + (i // z % 2) * 2 + i // (2 * z)
+    ).astype(BF16)
+    if len(lat.shape) == 3:
+        strips, per, _ = lat.shape
+        tokens = lat[...].reshape(strips * per, split)
+        n, cols = strips * per, 4
+        order = ones_where(
+            (n, n),
+            lambda i, j: j == (i // cols % strips) * per + i // (cols * strips) * cols + i % cols,
+        ).astype(BF16)
+        tokens = jnp.dot(order, tokens, preferred_element_type=F32).astype(BF16)
+    else:
+        tokens = lat[...]
+    tokens = jnp.dot(tokens, perm, preferred_element_type=F32)
+    own = noisy[...].astype(F32).T
+    lhs = jnp.concatenate([own, tokens, mask[...].astype(F32)], axis=1).astype(BF16)
     total = None
     for k in range(0, width, step):
         at = slice(k, k + step)
-        part = jnp.dot(noisy[...], pw[:, at], preferred_element_type=F32)
-        part = part + jnp.dot(tokens, cw[:split, at], preferred_element_type=F32)
-        part = part + jnp.dot(mask[...], cw[split:, at], preferred_element_type=F32)
+        part = jnp.dot(lhs, both[:, at], preferred_element_type=F32)
         part = part + (pb[:, at] + cb[:, at])
         comb[:, at] = part
         term = jnp.sum(part, axis=-1, keepdims=True)
@@ -298,16 +349,14 @@
     rows = half * columns
     chunks = half // 2 // shard_rows
     chunk_tokens = shard_rows * (columns // 2)
-    weight = fold_weights(conv_weight, mean_weight)
-    bias = jnp.dot(conv_bias[None], mean_weight, precision=lax.Precision.HIGHEST) + mean_bias
-    bias = jnp.tile(bias, (1, 128 // z))
     vmem = pl.BlockSpec(memory_space=pltpu.VMEM)
     arrived = pl.pallas_call(
         functools.partial(head_kernel, (n_c, n_s, n_t, shard_rows)),
         out_shape=jax.ShapeDtypeStruct((n_s, chunk_tokens, 4 * z), BF16),
-        in_specs=[pl.BlockSpec(memory_space=pl.ANY), vmem, vmem, vmem],
+        in_specs=[pl.BlockSpec(memory_space=pl.ANY)] + [vmem] * 5,
         out_specs=vmem,
         scratch_shapes=[
+            pltpu.VMEM((frames * K, 16 * z, channels), BF16),
             pltpu.VMEM((frames, half + 2, columns, channels), BF16),
             pltpu.VMEM((frames, (half + 2) * columns, channels), F32),
             pltpu.VMEM((rows, 128), F32),
@@ -328,26 +377,41 @@
         ],
         compiler_params=pltpu.CompilerParams(collective_id=0, has_side_effects=True),
         name="head",
-    )(section_input, weight, norm_gain[None], bias)
-    lat = arrived.reshape(n_s, shard_rows, columns // 2, 4 * z).transpose(1, 0, 2, 3)
-    lat = lat.reshape(tokens, 4 * z)
-
+    )(
+        section_input, conv_weight.T, norm_gain[None], mean_weight.T, conv_bias[None], mean_bias[None]
+    )
     width = patch_weight.shape[1]
-    block = min(tokens, 128)
+    block = min(tokens, 256)
+    per = block // n_s
+    if per % 16 == 0 and columns == 8:
+        lat = arrived
+        lat_spec = pl.BlockSpec((n_s, per, 4 * z), lambda i: (0, i, 0))
+    else:
+        lat = arrived.reshape(n_s, shard_rows, columns // 2, 4 * z).transpose(1, 0, 2, 3)
+        lat = lat.reshape(tokens, 4 * z)
+        lat_spec = pl.BlockSpec((block, 4 * z), lambda i: (i, 0))
     tok = lambda n: pl.BlockSpec((block, n), lambda i: (i, 0))
     full = lambda a: pl.BlockSpec(a.shape, lambda i: (0, 0))
+    hbm = pl.BlockSpec(memory_space=pl.ANY)
+    depth = patch_weight.shape[0] + context_weight.shape[0]
     vecs = [v[None] for v in (patch_bias, context_bias, norm_shift, norm_scale)]
     return pl.pallas_call(
         tail_kernel,
         out_shape=jax.ShapeDtypeStruct((tokens, width), BF16),
         grid=(tokens // block,),
-        in_specs=[tok(noisy_tokens.shape[1]), tok(mask_tokens.shape[1]), tok(4 * z)]
-        + [full(a) for a in (patch_weight, context_weight)]
+        in_specs=[
+            pl.BlockSpec((noisy_tokens.shape[1], block), lambda i: (0, i)),
+            tok(mask_tokens.shape[1]), lat_spec, hbm, hbm,
+        ]
         + [full(v) for v in vecs],
         out_specs=tok(width),
-        scratch_shapes=[pltpu.VMEM((block, width), F32)],
+        scratch_shapes=[
+            pltpu.VMEM((block, width), F32),
+            pltpu.VMEM((depth, width), BF16),
+            pltpu.SemaphoreType.DMA((2,)),
+        ],
         name="tail",
-    )(noisy_tokens, mask_tokens, lat, patch_weight, context_weight, *vecs)
+    )(noisy_tokens.T, mask_tokens, lat, patch_weight, context_weight, *vecs)
 
 
 def solution(mesh):

time: 50.3 us -> 31 us (0.62)
  other arithmetic: 7.84 us -> 0 us
  matrix products: 5.93 us -> 0 us
  local copies, waits for them, and re-layouts: 4.93 us -> 1.24 us
  Pallas kernels: 31.2 us -> 29.5 us
    select_n x1 -> x0, other arithmetic: 7.74 us -> none  [fold_weights(): jnp.where(keep, wide[None], jnp.zeros((), BF16)).reshape(taps * zo, width)]
    dot_general x5 -> x0, matrix products: 5.93 us -> none  [the longest x2 3.92 us: fold_weights(): term = jnp.dot(conv_weight, mat, preferred_element_type=F32)]
    reshape x1 -> x0, local copies, waits for them, and re-layouts: 1.61 us -> none  [body(): arrived.reshape(n_s, shard_rows, columns // 2, 4 * z).transpose(1, 0, 2, 3)]
    pallas_call x1, Pallas kernels: 11.9 us -> 10.3 us  [body(): pl.pallas_call(tail_kernel, out_shape=jax.ShapeDtypeStruct((tokens, width...]
    iota x15 -> x0, local copies, waits for them, and re-layouts: 1.1 us -> none  [fold_weights(): row = lax.broadcasted_iota(jnp.int32, (taps, zo, width), 0)]
    unnamed x13 -> x0, local copies, waits for them, and re-layouts: 0.79 us -> none
    broadcast_in_dim x1, local copies, waits for them, and re-layouts: 0.58 us -> 1.24 us  [body(): norm_gain[None]]
    another operation x2 -> x0, local copies, waits for them, and re-layouts: 0.58 us -> none  [body(): bias = jnp.tile(bias, (1, 128 // z))]
where the time goes in v2:
time: 31 us; the launch traced here: 30.8 us
  Pallas kernels  29.5 us (95%)
  local copies, waits for them, and re-layouts  1.24 us (4%)
    pallas_call x1, Pallas kernels, body(): pl.pallas_call(functools.partial(head_kernel, (n_c, n_s, n_t, shard_rows)...  19.2 us
    pallas_call x1, Pallas kernels, body(): pl.pallas_call(tail_kernel, out_shape=jax.ShapeDtypeStruct((tokens, width...  10.3 us
    broadcast_in_dim x1, local copies, waits for them, and re-layouts, body(): norm_gain[None]  1.24 us

profile of v2, /device:TPU:0, one launch (start us, length us, event | category | flops | bytes accessed | tf_op | source)
XLA Modules:
  0.0 30.8 jit_solution(3689638980983511168)
XLA Ops:
  0.0 1.2 %broadcast_in_dim.21.gain_ref = f32[1,384]{1,0:T(1,128)} reshape(f32[384]{0:T(512)} %param.15) | data formatting | bytes 3072 | tf_op jit(solution)/shard_map/broadcast_in_dim | solution.py:381
  1.2 19.2 %head.1.lat = bf16[8,64,64]{2,1,0:T(8,128)(2,1)} custom-call(bf16[2,128,8,384]{3,2,1,0:T(8,128)(2,1)} %x_hbm.1, bf16[864,384]{1,0:T(8,128)(2,1)} %bitcast.9, f32[1,384]{1,0:T(1,128)} %broadcast_in_dim.21.gain_ref, f32[16,32]{1,0:T(8,128)} %bitcast.15, f32[1,32]{1,0:T(1,128)} %bitcast.16, f32[1,16]{1,0:T(1,128)} %bitcast.17), custom_call_target="tpu_custom_call" | custom-call | tf_op jit(solution)/shard_map/head/pallas_call | solution.py:353
  20.4 10.3 %tail.1 = bf16[512,5120]{1,0:T(8,128)(2,1)} custom-call(bf16[64,512]{1,0:T(8,128)(2,1)} %bitcast.10, bf16[512,128]{1,0:T(8,128)(2,1)} %mask.1, bf16[8,64,64]{2,1,0:T(8,128)(2,1)} %head.1.lat, bf16[64,5120]{1,0:T(8,128)(2,1)} %pw.1, bf16[192,5120]{1,0:T(8,128)(2,1)} %cw.1, f32[1,5120]{1,0:T(1,128)} %bitcast.11, f32[1,5120]{1,0:T(1,128)} %bitcast.12, ...), custom_call_target="tpu_custom_call" | custom-call | tf_op jit(solution)/shard_map/tail/pallas_call | solution.py:398

commit v3 on v2

--- a/solution.py
+++ b/solution.py
@@ -40,12 +40,14 @@
     for part in (high, low):
         tall = jnp.dot(spread, part, preferred_element_type=F32).astype(BF16)
         parts.append((jnp.dot(tall, copier, preferred_element_type=F32) * keep).astype(BF16))
+    parts = jnp.concatenate(parts, axis=0)
     nothing = jnp.zeros((z, wt.shape[2]), BF16)
     for a in range(K):
         for b in range(K):
             at = (a * K + b) * K * zo
             rhs = cw_ref[at : at + K * zo, :]
-            res = sum(jnp.dot(p, rhs, preferred_element_type=F32) for p in parts).astype(BF16)
+            res = jnp.dot(parts, rhs, preferred_element_type=F32)
+            res = (res[: 4 * z] + res[4 * z :]).astype(BF16)
             for f in range(2):
                 for slot in range(4):
                     row = slot * 4 * z + (f + 2 - a) * z
@@ -136,7 +138,7 @@
         xin[:, half + 1 : half + 2] = zero_row
 
     load.wait()
-    gain = gain_ref[...]
+    gain = gain_ref[...].reshape(1, channels)
     step_rows = 6 if (half + 2) % 6 == 0 else 2
     for f in range(frames):
 
@@ -284,7 +286,7 @@
             away.wait_send()
 
 
-def tail_kernel(noisy, mask, lat, pw, cw, pb, cb, shift, scale, out, comb, both, sems):
+def tail_kernel(noisy, mask, lat, pw, cw, pb, cb, shift, scale, out, comb, both, inv_ref, mean_ref, sems):
     split = lat.shape[-1]
     width = comb.shape[1]
     step = 512
@@ -299,41 +301,50 @@
         upper.wait()
         lower.wait()
 
-    perm = ones_where(
-        (split, split), lambda i, j: j == (i % z) * 4 + (i // z % 2) * 2 + i // (2 * z)
-    ).astype(BF16)
-    if len(lat.shape) == 3:
-        strips, per, _ = lat.shape
-        tokens = lat[...].reshape(strips * per, split)
-        n, cols = strips * per, 4
-        order = ones_where(
-            (n, n),
-            lambda i, j: j == (i // cols % strips) * per + i // (cols * strips) * cols + i % cols,
+    parts = comb.shape[0] // out.shape[0]
+
+    @pl.when(pl.program_id(0) % parts == 0)
+    def _():
+        perm = ones_where(
+            (split, split), lambda i, j: j == (i % z) * 4 + (i // z % 2) * 2 + i // (2 * z)
         ).astype(BF16)
-        tokens = jnp.dot(order, tokens, preferred_element_type=F32).astype(BF16)
-    else:
-        tokens = lat[...]
-    tokens = jnp.dot(tokens, perm, preferred_element_type=F32)
-    own = noisy[...].astype(F32).T
-    lhs = jnp.concatenate([own, tokens, mask[...].astype(F32)], axis=1).astype(BF16)
-    total = None
+        if len(lat.shape) == 3:
+            strips, per, _ = lat.shape
+            tokens = lat[...].reshape(strips * per, split)
+            n, cols = strips * per, 4
+            order = ones_where(
+                (n, n),
+                lambda i, j: j == (i // cols % strips) * per + i // (cols * strips) * cols + i % cols,
+            ).astype(BF16)
+            tokens = jnp.dot(order, tokens, preferred_element_type=F32).astype(BF16)
+        else:
+            tokens = lat[...]
+        tokens = jnp.dot(tokens, perm, preferred_element_type=F32)
+        own = noisy[...].astype(F32).T
+        lhs = jnp.concatenate([own, tokens, mask[...].astype(F32)], axis=1).astype(BF16)
+        total = None
+        for k in range(0, width, step):
+            at = slice(k, k + step)
+            part = jnp.dot(lhs, both[:, at], preferred_element_type=F32)
+            part = part + (pb[:, at] + cb[:, at])
+            comb[:, at] = part
+            term = jnp.sum(part, axis=-1, keepdims=True)
+            total = term if total is None else total + term
+        mean = total * (1.0 / width)
+        square = None
+        for k in range(0, width, step):
+            d = comb[:, k : k + step] - mean
+            term = jnp.sum(d * d, axis=-1, keepdims=True)
+            square = term if square is None else square + term
+        mean_ref[...] = jnp.broadcast_to(mean, mean_ref.shape)
+        inv_ref[...] = jnp.broadcast_to(lax.rsqrt(square * (1.0 / width) + 1e-06), inv_ref.shape)
+
+    rows = out.shape[0]
+    mine = pl.ds(pl.multiple_of(pl.program_id(0) % parts * rows, rows), rows)
+    mean, inv = mean_ref[mine, :1], inv_ref[mine, :1]
     for k in range(0, width, step):
         at = slice(k, k + step)
-        part = jnp.dot(lhs, both[:, at], preferred_element_type=F32)
-        part = part + (pb[:, at] + cb[:, at])
-        comb[:, at] = part
-        term = jnp.sum(part, axis=-1, keepdims=True)
-        total = term if total is None else total + term
-    mean = total * (1.0 / width)
-    square = None
-    for k in range(0, width, step):
-        d = comb[:, k : k + step] - mean
-        term = jnp.sum(d * d, axis=-1, keepdims=True)
-        square = term if square is None else square + term
-    inv = lax.rsqrt(square * (1.0 / width) + 1e-06)
-    for k in range(0, width, step):
-        at = slice(k, k + step)
-        out[:, at] = ((comb[:, at] - mean) * inv * (1.0 + scale[:, at]) + shift[:, at]).astype(BF16)
+        out[:, at] = ((comb[mine, at] - mean) * inv * (1.0 + scale[:, at]) + shift[:, at]).astype(BF16)
 
 
 def body(
@@ -353,7 +364,7 @@
     arrived = pl.pallas_call(
         functools.partial(head_kernel, (n_c, n_s, n_t, shard_rows)),
         out_shape=jax.ShapeDtypeStruct((n_s, chunk_tokens, 4 * z), BF16),
-        in_specs=[pl.BlockSpec(memory_space=pl.ANY)] + [vmem] * 5,
+        in_specs=[pl.BlockSpec(memory_space=pltpu.HBM)] + [vmem] * 5,
         out_specs=vmem,
         scratch_shapes=[
             pltpu.VMEM((frames * K, 16 * z, channels), BF16),
@@ -375,22 +386,25 @@
             pltpu.SemaphoreType.DMA((frames * chunks * n_c,)),
             pltpu.SemaphoreType.DMA((n_s,)),
         ],
-        compiler_params=pltpu.CompilerParams(collective_id=0, has_side_effects=True),
+        compiler_params=pltpu.CompilerParams(
+            collective_id=0, has_side_effects=True, vmem_limit_bytes=20 * 2**20
+        ),
         name="head",
     )(
-        section_input, conv_weight.T, norm_gain[None], mean_weight.T, conv_bias[None], mean_bias[None]
+        section_input, conv_weight.T, norm_gain, mean_weight.T, conv_bias[None], mean_bias[None]
     )
     width = patch_weight.shape[1]
     block = min(tokens, 256)
     per = block // n_s
     if per % 16 == 0 and columns == 8:
         lat = arrived
-        lat_spec = pl.BlockSpec((n_s, per, 4 * z), lambda i: (0, i, 0))
+        lat_spec = pl.BlockSpec((n_s, per, 4 * z), lambda i: (0, i // parts, 0))
     else:
         lat = arrived.reshape(n_s, shard_rows, columns // 2, 4 * z).transpose(1, 0, 2, 3)
         lat = lat.reshape(tokens, 4 * z)
-        lat_spec = pl.BlockSpec((block, 4 * z), lambda i: (i, 0))
-    tok = lambda n: pl.BlockSpec((block, n), lambda i: (i, 0))
+        lat_spec = pl.BlockSpec((block, 4 * z), lambda i: (i // parts, 0))
+    parts = 2 if block % 32 == 0 else 1
+    tok = lambda n: pl.BlockSpec((block, n), lambda i: (i // parts, 0))
     full = lambda a: pl.BlockSpec(a.shape, lambda i: (0, 0))
     hbm = pl.BlockSpec(memory_space=pl.ANY)
     depth = patch_weight.shape[0] + context_weight.shape[0]
@@ -398,18 +412,21 @@
     return pl.pallas_call(
         tail_kernel,
         out_shape=jax.ShapeDtypeStruct((tokens, width), BF16),
-        grid=(tokens // block,),
+        grid=(tokens // block * parts,),
         in_specs=[
-            pl.BlockSpec((noisy_tokens.shape[1], block), lambda i: (0, i)),
+            pl.BlockSpec((noisy_tokens.shape[1], block), lambda i: (0, i // parts)),
             tok(mask_tokens.shape[1]), lat_spec, hbm, hbm,
         ]
         + [full(v) for v in vecs],
-        out_specs=tok(width),
+        out_specs=pl.BlockSpec((block // parts, width), lambda i: (i, 0)),
         scratch_shapes=[
             pltpu.VMEM((block, width), F32),
             pltpu.VMEM((depth, width), BF16),
+            pltpu.VMEM((block, 128), F32),
+            pltpu.VMEM((block, 128), F32),
             pltpu.SemaphoreType.DMA((2,)),
         ],
+        compiler_params=pltpu.CompilerParams(vmem_limit_bytes=28 * 2**20),
         name="tail",
     )(noisy_tokens.T, mask_tokens, lat, patch_weight, context_weight, *vecs)
 

time: 31 us -> 32.4 us (1.045)
  local copies, waits for them, and re-layouts: 1.24 us -> 6.44 us
  Pallas kernels: 29.5 us -> 25.6 us
    unnamed x0 -> x28, local copies, waits for them, and re-layouts: none -> 6.44 us
    pallas_call x1, Pallas kernels: 10.3 us -> 8.12 us  [body(): pl.pallas_call(tail_kernel, out_shape=jax.ShapeDtypeStruct((tokens, width...]
    pallas_call x1, Pallas kernels: 19.2 us -> 17.5 us  [body(): pl.pallas_call(functools.partial(head_kernel, (n_c, n_s, n_t, shard_rows)...]
    broadcast_in_dim x1 -> x0, local copies, waits for them, and re-layouts: 1.24 us -> none  [body(): norm_gain[None]]
where the time goes in v3:
time: 32.4 us; the launch traced here: 32.2 us
  Pallas kernels  25.6 us (79%)
  local copies, waits for them, and re-layouts  6.44 us (20%)
    pallas_call x1, Pallas kernels, body(): pl.pallas_call(functools.partial(head_kernel, (n_c, n_s, n_t, shard_rows)...  17.5 us
    pallas_call x1, Pallas kernels, body(): pl.pallas_call(tail_kernel, out_shape=jax.ShapeDtypeStruct((tokens, width...  8.12 us
    unnamed x28, local copies, waits for them, and re-layouts  6.44 us

profile of v3, /device:TPU:0, one launch (start us, length us, event | category | flops | bytes accessed | tf_op | source)
XLA Modules:
  0.0 32.2 jit_solution(12210628040871477105)
XLA Ops:
  0.0 0.0 copy-start
  0.0 0.0 copy-start.1
  0.0 1.5 %copy-done.1 = bf16[2,128,8,384]{3,2,1,0:T(8,128)(2,1)S(1)} copy-done((bf16[2,128,8,384]{3,2,1,0:T(8,128)(2,1)S(1)}, bf16[2,128,8,384]{3,2,1,0:T(8,128)(2,1)}, u32[]{:S(2)}) %copy-start.1) | copy-done | bytes 1572888
  1.6 0.0 copy-start.2
  1.6 1.1 %copy-done.2 = bf16[384,864]{0,1:T(8,128)(2,1)S(1)} copy-done((bf16[384,864]{0,1:T(8,128)(2,1)S(1)}, bf16[384,864]{0,1:T(8,128)(2,1)}, u32[]{:S(2)}) %copy-start.2) | copy-done | bytes 663576
  2.6 0.0 copy-start.10
  2.6 0.7 %copy-done.10 = f32[32,16]{0,1:T(8,128)S(1)} copy-done((f32[32,16]{0,1:T(8,128)S(1)}, f32[32,16]{0,1:T(8,128)}, u32[]{:S(2)}) %copy-start.10) | copy-done | bytes 2072
  3.3 0.0 copy-start.11
  3.3 0.7 %copy-done.11 = f32[384]{0:T(512)S(1)} copy-done((f32[384]{0:T(512)S(1)}, f32[384]{0:T(512)}, u32[]{:S(2)}) %copy-start.11) | copy-done | bytes 1560
  4.0 0.0 copy-start.12
  4.0 0.7 %copy-done.12 = f32[32]{0:T(128)S(1)} copy-done((f32[32]{0:T(128)S(1)}, f32[32]{0:T(128)}, u32[]{:S(2)}) %copy-start.12) | copy-done | bytes 152
  4.7 0.0 copy-start.13
  4.7 0.7 %copy-done.13 = f32[16]{0:T(128)S(1)} copy-done((f32[16]{0:T(128)S(1)}, f32[16]{0:T(128)}, u32[]{:S(2)}) %copy-start.13) | copy-done | bytes 88
  5.3 0.0 copy-start.4
  5.3 0.0 copy-start.5
  5.3 0.0 copy-start.6
  5.3 0.0 copy-start.7
  5.3 0.0 copy-start.8
  5.4 0.0 copy-start.9
  5.4 17.5 %head.1.lat = bf16[8,64,64]{2,1,0:T(8,128)(2,1)S(1)} custom-call(bf16[2,128,8,384]{3,2,1,0:T(8,128)(2,1)S(1)} %copy-done.1, bf16[864,384]{1,0:T(8,128)(2,1)S(1)} %bitcast.9, f32[384]{0:T(512)S(1)} %copy-done.11, f32[16,32]{1,0:T(8,128)S(1)} %bitcast.15, f32[1,32]{1,0:T(1,128)S(1)} %bitcast.16, f32[1,16]{1,0:T(1,128)S(1)} %bitcast.17), custom_call_target="tpu_custom_call" | custom-call | tf_op jit(solution)/shard_map/head/pallas_call | solution.py:364
  22.9 0.0 copy-done
  22.9 0.0 copy-done.4
  22.9 0.0 copy-done.5
  22.9 0.0 copy-done.6
  22.9 0.0 copy-done.7
  23.0 0.0 copy-done.8
  23.0 0.0 copy-done.9
  23.0 0.0 copy-start.3
  23.0 1.1 %copy-done.3 = bf16[64,5120]{1,0:T(8,128)(2,1)S(1)} copy-done((bf16[64,5120]{1,0:T(8,128)(2,1)S(1)}, bf16[64,5120]{1,0:T(8,128)(2,1)}, u32[]{:S(2)}) %copy-start.3) | copy-done | bytes 655384
  24.1 8.1 %tail.1 = bf16[512,5120]{1,0:T(8,128)(2,1)} custom-call(bf16[64,512]{1,0:T(8,128)(2,1)S(1)} %bitcast.10, bf16[512,128]{1,0:T(8,128)(2,1)S(1)} %copy-done.4, bf16[8,64,64]{2,1,0:T(8,128)(2,1)S(1)} %head.1.lat, bf16[64,5120]{1,0:T(8,128)(2,1)S(1)} %copy-done.3, bf16[192,5120]{1,0:T(8,128)(2,1)S(1)} %copy-done, f32[1,5120]{1,0:T(1,128)S(1)} %bitcast.11, ...), custom_call_target="tpu_custom_call" | custom-call | tf_op jit(solution)/shard_map/tail/pallas_call | solution.py:412
Async XLA Ops:
  0.0 22.9 %copy-start = (bf16[192,5120]{1,0:T(8,128)(2,1)S(1)}, bf16[192,5120]{1,0:T(8,128)(2,1)}, u32[]{:S(2)}) copy-start(bf16[192,5120]{1,0:T(8,128)(2,1)} %cw.1) | copy-start | bytes 5898244
  0.0 1.6 %copy-start.1 = (bf16[2,128,8,384]{3,2,1,0:T(8,128)(2,1)S(1)}, bf16[2,128,8,384]{3,2,1,0:T(8,128)(2,1)}, u32[]{:S(2)}) copy-start(bf16[2,128,8,384]{3,2,1,0:T(8,128)(2,1)} %x_hbm.1) | copy-start | bytes 4718596
  1.6 1.1 %copy-start.2 = (bf16[384,864]{0,1:T(8,128)(2,1)S(1)}, bf16[384,864]{0,1:T(8,128)(2,1)}, u32[]{:S(2)}) copy-start(bf16[384,864]{0,1:T(8,128)(2,1)} %param.16) | copy-start | bytes 1990660
  2.6 0.7 %copy-start.10 = (f32[32,16]{0,1:T(8,128)S(1)}, f32[32,16]{0,1:T(8,128)}, u32[]{:S(2)}) copy-start(f32[32,16]{0,1:T(8,128)} %param.18) | copy-start | bytes 6148
  3.3 0.7 %copy-start.11 = (f32[384]{0:T(512)S(1)}, f32[384]{0:T(512)}, u32[]{:S(2)}) copy-start(f32[384]{0:T(512)} %gain_ref.1) | copy-start | bytes 4612
  4.0 0.7 %copy-start.12 = (f32[32]{0:T(128)S(1)}, f32[32]{0:T(128)}, u32[]{:S(2)}) copy-start(f32[32]{0:T(128)} %param.17) | copy-start | bytes 388
  4.7 0.7 %copy-start.13 = (f32[16]{0:T(128)S(1)}, f32[16]{0:T(128)}, u32[]{:S(2)}) copy-start(f32[16]{0:T(128)} %param.19) | copy-start | bytes 196
  5.3 17.6 %copy-start.4 = (bf16[512,128]{1,0:T(8,128)(2,1)S(1)}, bf16[512,128]{1,0:T(8,128)(2,1)}, u32[]{:S(2)}) copy-start(bf16[512,128]{1,0:T(8,128)(2,1)} %mask.1) | copy-start | bytes 393220
  5.3 17.6 %copy-start.5 = (bf16[512,64]{0,1:T(8,128)(2,1)S(1)}, bf16[512,64]{0,1:T(8,128)(2,1)}, u32[]{:S(2)}) copy-start(bf16[512,64]{0,1:T(8,128)(2,1)} %param.20) | copy-start | bytes 196612
  5.3 17.6 %copy-start.6 = (f32[5120]{0:T(1024)S(1)}, f32[5120]{0:T(1024)}, u32[]{:S(2)}) copy-start(f32[5120]{0:T(1024)} %param.23) | copy-start | bytes 61444
  5.3 17.6 %copy-start.7 = (f32[5120]{0:T(1024)S(1)}, f32[5120]{0:T(1024)}, u32[]{:S(2)}) copy-start(f32[5120]{0:T(1024)} %param.25) | copy-start | bytes 61444
  5.3 17.6 %copy-start.8 = (f32[5120]{0:T(1024)S(1)}, f32[5120]{0:T(1024)}, u32[]{:S(2)}) copy-start(f32[5120]{0:T(1024)} %param.26) | copy-start | bytes 61444
  5.4 17.6 %copy-start.9 = (f32[5120]{0:T(1024)S(1)}, f32[5120]{0:T(1024)}, u32[]{:S(2)}) copy-start(f32[5120]{0:T(1024)} %param.27) | copy-start | bytes 61444
  23.0 1.1 %copy-start.3 = (bf16[64,5120]{1,0:T(8,128)(2,1)S(1)}, bf16[64,5120]{1,0:T(8,128)(2,1)}, u32[]{:S(2)}) copy-start(bf16[64,5120]{1,0:T(8,128)(2,1)} %pw.1) | copy-start | bytes 1966084

commit v4 on v3

--- a/solution.py
+++ b/solution.py
@@ -386,9 +386,7 @@
             pltpu.SemaphoreType.DMA((frames * chunks * n_c,)),
             pltpu.SemaphoreType.DMA((n_s,)),
         ],
-        compiler_params=pltpu.CompilerParams(
-            collective_id=0, has_side_effects=True, vmem_limit_bytes=20 * 2**20
-        ),
+        compiler_params=pltpu.CompilerParams(collective_id=0, has_side_effects=True),
         name="head",
     )(
         section_input, conv_weight.T, norm_gain, mean_weight.T, conv_bias[None], mean_bias[None]
@@ -426,7 +424,6 @@
             pltpu.VMEM((block, 128), F32),
             pltpu.SemaphoreType.DMA((2,)),
         ],
-        compiler_params=pltpu.CompilerParams(vmem_limit_bytes=28 * 2**20),
         name="tail",
     )(noisy_tokens.T, mask_tokens, lat, patch_weight, context_weight, *vecs)
 

time: 32.4 us -> 29.8 us (0.920)
  local copies, waits for them, and re-layouts: 6.44 us -> 0 us
  Pallas kernels: 25.6 us -> 29.4 us
    unnamed x28 -> x0, local copies, waits for them, and re-layouts: 6.44 us -> none
    pallas_call x1, Pallas kernels: 8.12 us -> 10.3 us  [body(): pl.pallas_call(tail_kernel, out_shape=jax.ShapeDtypeStruct((tokens, width...]
    pallas_call x1, Pallas kernels: 17.5 us -> 19.2 us  [body(): pl.pallas_call(functools.partial(head_kernel, (n_c, n_s, n_t, shard_rows)...]
where the time goes in v4:
time: 29.8 us; the launch traced here: 29.4 us
  Pallas kernels  29.4 us (99%)
    pallas_call x1, Pallas kernels, body(): pl.pallas_call(functools.partial(head_kernel, (n_c, n_s, n_t, shard_rows)...  19.2 us
    pallas_call x1, Pallas kernels, body(): pl.pallas_call(tail_kernel, out_shape=jax.ShapeDtypeStruct((tokens, width...  10.3 us

profile of v4, /device:TPU:0, one launch (start us, length us, event | category | flops | bytes accessed | tf_op | source)
XLA Modules:
  0.0 29.4 jit_solution(1773321439932648634)
XLA Ops:
  0.0 19.2 %head.1.lat = bf16[8,64,64]{2,1,0:T(8,128)(2,1)} custom-call(bf16[2,128,8,384]{3,2,1,0:T(8,128)(2,1)} %x_hbm.1, bf16[864,384]{1,0:T(8,128)(2,1)} %bitcast.9, f32[384]{0:T(512)} %gain_ref.1, f32[16,32]{1,0:T(8,128)} %bitcast.15, f32[1,32]{1,0:T(1,128)} %bitcast.16, f32[1,16]{1,0:T(1,128)} %bitcast.17), custom_call_target="tpu_custom_call" | custom-call | tf_op jit(solution)/shard_map/head/pallas_call | solution.py:364
  19.2 10.3 %tail.1 = bf16[512,5120]{1,0:T(8,128)(2,1)} custom-call(bf16[64,512]{1,0:T(8,128)(2,1)} %bitcast.10, bf16[512,128]{1,0:T(8,128)(2,1)} %mask.1, bf16[8,64,64]{2,1,0:T(8,128)(2,1)} %head.1.lat, bf16[64,5120]{1,0:T(8,128)(2,1)} %pw.1, bf16[192,5120]{1,0:T(8,128)(2,1)} %cw.1, f32[1,5120]{1,0:T(1,128)} %bitcast.11, f32[1,5120]{1,0:T(1,128)} %bitcast.12, ...), custom_call_target="tpu_custom_call" | custom-call | tf_op jit(solution)/shard_map/tail/pallas_call | solution.py:410
